TPU v7x, 32 devices: a whole 2x2x4 slice. The times are simulated.
32 devices in a mesh: group: 2 (over core), dp: 4 (over z), section: 2 (over x), tensor: 2 (over y).
Axes of the slice: x: 2, y: 2, z: 4, core: 2. Of those that a mesh axis runs over, the one named last changes fastest.
Arguments:
- merged: bfloat16 [768, 5120], P('dp'), may hold values from -6 to 6
- counts: int32 [8], P('dp'), may hold values from 4 to 384
- owners: int32 [768, 1], P('dp'), may hold values from 0 to 3; in each aligned block of 192 rows (0 to 191, 192 to 383, ...) at most 96 rows name the same one
- w_merge: bfloat16 [5120, 8192], P(None, ('group', 'section', 'tensor')), may hold values from -0.078125 to 0.078125
- norm_gain: float32 [8192], P(('group', 'section', 'tensor')), may hold values from 0.25 to 1.75
- cotangent: bfloat16 [4, 4, 96, 8192], P('dp', None, None, ('group', 'section', 'tensor')), may hold values from -6 to 6
Outputs:
- embedded: bfloat16 [4, 4, 96, 8192], P('dp', None, None, ('group', 'section', 'tensor'))
- grad_merged: float32 [768, 5120], P('dp', ('group', 'section', 'tensor'))
- grad_weight: float32 [5120, 8192], P('dp', ('group', 'section', 'tensor'))
Inputs may be any that keep to these rules, and one draw needn't show every extreme that they name: `owners`: in each replica's 192 rows no owner appears more than 96 times.
All inputs are finite; a program needn't handle non-finite values.
Results may differ from a plain program's by a relative error of at most 0.0049.
Values may be sent and summed in bfloat16 or wider, within the bound.
A program may use at most 64 MiB of HBM per device.

v0:
```python
import jax
import jax.numpy as jnp
from jax import lax
from jax.sharding import PartitionSpec as P

D = 8192


def on_device(merged, counts, owners, w_merge, norm_gain, cotangent):
    rows = merged.shape[0]
    columns = w_merge.shape[1]
    replicas = lax.axis_size("dp")
    slots = cotangent.shape[2]
    images = counts.shape[0]
    per_image = rows // images
    projected = jnp.dot(merged, w_merge, preferred_element_type=jnp.float32).astype(jnp.bfloat16)
    row_index = jnp.arange(rows, dtype=jnp.int32)
    image_of = row_index // per_image
    picked = image_of[:, None] == jnp.arange(images, dtype=jnp.int32)[None, :]
    count_of = jnp.sum(jnp.where(picked, counts[None, :], 0), axis=1)
    valid = (4 * (row_index % per_image) < count_of).astype(jnp.float32)
    masked = (projected.astype(jnp.float32) * valid[:, None]).astype(jnp.bfloat16)
    owner = owners[:, 0]
    hits = (owner[:, None] == jnp.arange(replicas, dtype=jnp.int32)[None, :]).astype(jnp.int32)
    before = jnp.cumsum(hits, axis=0) - hits
    slot_index = jnp.sum(before * hits, axis=1)
    target = owner * slots + slot_index
    placer = (jnp.arange(replicas * slots, dtype=jnp.int32)[:, None] == target[None, :]).astype(
        jnp.bfloat16
    )
    outgoing = jnp.dot(placer, masked, preferred_element_type=jnp.float32).astype(jnp.bfloat16)
    outgoing = outgoing.reshape(replicas, slots, columns)
    received = lax.all_to_all(outgoing, "dp", split_axis=0, concat_axis=0, tiled=True)
    values = received.astype(jnp.float32)
    square_sums = lax.psum(jnp.sum(values * values, axis=2), ("group", "section", "tensor"))
    scale = lax.rsqrt(square_sums / D + 1e-05)
    normed = (values * scale[:, :, None] * norm_gain[None, None, :]).astype(jnp.bfloat16)
    embedded = normed[None]
    grad_in = cotangent[0].astype(jnp.float32) * norm_gain[None, None, :]
    inner_sums = lax.psum(jnp.sum(grad_in * values, axis=2), ("group", "section", "tensor"))
    inner = inner_sums / D
    slot_grad = (scale[:, :, None] * grad_in - values * (scale**3 * inner)[:, :, None]).astype(
        jnp.bfloat16
    )
    returned = lax.all_to_all(slot_grad, "dp", split_axis=0, concat_axis=0, tiled=True)
    returned = returned.reshape(replicas * slots, columns)
    gathered = lax.dot_general(
        placer, returned, (((0,), (0,)), ((), ())), preferred_element_type=jnp.float32
    )
    back = (gathered * valid[:, None]).astype(jnp.bfloat16)
    input_terms = lax.dot_general(
        back, w_merge, (((1,), (1,)), ((), ())), preferred_element_type=jnp.float32
    )
    grad_merged = lax.psum_scatter(
        input_terms, ("group", "section", "tensor"), scatter_dimension=1, tiled=True
    )
    column_block = lax.all_to_all(merged, "dp", split_axis=1, concat_axis=0, tiled=True)
    grad_weight = lax.dot_general(
        column_block,
        lax.all_gather(back, "dp", axis=0, tiled=True),
        (((0,), (0,)), ((), ())),
        preferred_element_type=jnp.float32,
    )
    return (embedded, grad_merged, grad_weight)


def solution(mesh):
    placed = (
        P("dp", None),
        P("dp"),
        P("dp", None),
        P(None, ("group", "section", "tensor")),
        P(("group", "section", "tensor")),
        P("dp", None, None, ("group", "section", "tensor")),
    )
    return jax.shard_map(
        on_device,
        mesh=mesh,
        in_specs=placed,
        out_specs=(
            P("dp", None, None, ("group", "section", "tensor")),
            P("dp", ("group", "section", "tensor")),
            P("dp", ("group", "section", "tensor")),
        ),
        check_vma=False,
    )
```

profile of v0, /device:TPU:0, one launch (start us, length us, event | category | flops | bytes accessed | tf_op | source)
XLA Modules:
  0.0 182.4 jit_solution(6930971145670902794)
XLA Ops:
  8.0 0.0 all-gather.2.cloned.1.call-start
  8.1 0.7 iota_compare_fusion.3
  8.7 0.7 fusion.18
  9.5 1.2 reduce-window.6
  10.8 0.1 slice.12
  10.8 0.1 copy.23
  11.0 0.1 copy.24
  11.1 0.1 add_bitcast_fusion
  11.2 0.7 fusion.16
  11.9 0.7 multiply_add_fusion
  12.5 0.0 copy-start.2
  12.5 7.0 %convolution_convert_fusion = bf16[384,1024]{1,0:T(8,128)(2,1)S(1)} fusion(bf16[192,5120]{1,0:T(8,128)(2,1)} %param.6, bf16[5120,1024]{1,0:T(8,128)(2,1)} %param.9, f32[192]{0:T(256)S(1)} %compare_convert_fusion, s32[192]{0:T(256)S(1)} %multiply_add_fusion), kind=kOutput, calls=%fused_computation.14 | convolution fusion | flops 2165514240 | bytes 13239808 | tf_op jit(solution)/shard_map/dot_general | solution.py:31
  19.6 0.0 copy-start
  19.6 26.4 %all_to_all.29 = bf16[4,96,1024]{2,1,0:T(8,128)(2,1)S(1)} all-to-all(bf16[4,96,1024]{2,1,0:T(8,128)(2,1)S(1)} %bitcast.38), channel_id=1, replica_groups=mesh['group'=2,'dp'=4,'section'=2,'tensor'=2] {'dp'}, dimensions={0} | all-to-all | bytes 1572864 | tf_op jit(solution)/shard_map/all_to_all | solution.py:33
  46.0 0.0 copy-done.2
  46.0 0.0 copy-done
  46.0 0.4 fusion.3
  46.4 14.3 %all-reduce.1 = (f32[4,96]{1,0:T(4,128)S(1)}, f32[4,96]{1,0:T(4,128)S(1)}) all-reduce(f32[4,96]{1,0:T(4,128)S(1)} %get-tuple-element.19, f32[4,96]{1,0:T(4,128)S(1)} %get-tuple-element.18), channel_id=1, replica_groups=mesh['group'=2,'dp'=4,'section'=2,'tensor'=2] {'group','section','tensor'}, use_global_device_ids=true, to_apply=%region_5.6 | all-reduce | flops 768 | bytes 6144 | tf_op jit(solution)/shard_map/psum | solution.py:35
  60.7 1.4 fusion.5
  62.1 23.6 %all_to_all.30 = bf16[4,96,1024]{2,1,0:T(8,128)(2,1)S(1)} all-to-all(bf16[4,96,1024]{2,1,0:T(8,128)(2,1)S(1)} %get-tuple-element.22), channel_id=1, replica_groups=mesh['group'=2,'dp'=4,'section'=2,'tensor'=2] {'dp'}, dimensions={0} | all-to-all | bytes 1572864 | tf_op jit(solution)/shard_map/all_to_all | solution.py:45
  85.7 1.2 fusion.7
  86.9 0.0 all-gather.2.cloned.1.call-update
  86.9 0.0 reduce-scatter.2.cloned.1.call-start
  86.9 9.7 %fusion.21 = f32[192,5120]{1,0:T(8,128)} fusion(bf16[192,1024]{1,0:T(8,128)(2,1)} %fusion.7, bf16[5120,1024]{1,0:T(8,128)(2,1)} %param.9), kind=kOutput, calls=%fused_computation.48 | convolution fusion | flops 2013265920 | bytes 14811136 | tf_op jit(solution)/shard_map/dot_general | solution.py:51
  96.7 0.0 copy-start.1
  96.7 0.0 reduce-scatter.2.cloned.1.call-update
  96.7 1.5 copy-done.1
  98.2 0.1 copy.31
  98.3 64.7 %all_to_all.31 = bf16[192,4,1280]{2,0,1:T(8,128)(2,1)S(1)} all-to-all(bf16[192,4,1280]{2,0,1:T(8,128)(2,1)S(1)} %bitcast.34), channel_id=1, replica_groups=mesh['group'=2,'dp'=4,'section'=2,'tensor'=2] {'dp'}, dimensions={1} | all-to-all | bytes 3932160 | tf_op jit(solution)/shard_map/all_to_all | solution.py:57
  163.1 0.0 all-gather.2.cloned.1.call-done
  163.1 6.0 %convolution_bitcast_fusion = f32[1280,1024]{0,1:T(8,128)} fusion(bf16[768,1024]{1,0:T(8,128)(2,1)} %all-gather.2.cloned.1.call-done, bf16[768,1280]{1,0:T(8,128)(2,1)S(1)} %bitcast.37), kind=kOutput, calls=%fused_computation | convolution fusion | flops 2013265920 | bytes 8781824 | tf_op jit(solution)/shard_map/dot_general | solution.py:58
  169.1 5.9 %copy.26 = f32[1280,1024]{1,0:T(8,128)} copy(f32[1280,1024]{0,1:T(8,128)} %convolution_bitcast_fusion) | data formatting | bytes 10485760
  174.9 0.0 reduce-scatter.2.cloned.1.call-done
  (8 shorter events, 0.1 us)
Async XLA Ops:
  8.0 155.1 %all-gather.2.cloned.1.call-start = ((), (), s32[]{:S(2)}) async-start(), calls=%async_computation.5 | async-start | bytes 1966080 | tf_op jit(solution)/shard_map/all_gather | solution.py:60
  12.5 33.4 %copy-start.2 = (f32[1024]{0:T(1024)S(1)}, f32[1024]{0:T(1024)}, u32[]{:S(2)}) copy-start(f32[1024]{0:T(1024)} %param.10) | copy-start | bytes 12292
  19.6 26.4 %copy-start = (bf16[1,4,96,1024]{3,2,1,0:T(8,128)(2,1)S(1)}, bf16[1,4,96,1024]{3,2,1,0:T(8,128)(2,1)}, u32[]{:S(2)}) copy-start(bf16[1,4,96,1024]{3,2,1,0:T(8,128)(2,1)} %param.11) | copy-start | bytes 2359300
  86.9 88.1 %reduce-scatter.2.cloned.1.call-start = ((), (), s32[]{:S(2)}) async-start(), calls=%async_computation.4 | async-start | bytes 4423680 | tf_op jit(solution)/shard_map/reduce_scatter | solution.py:54
  96.7 1.5 copy-start.1
Sparse Core Ops, SparseCore 0:
  87.0 58.4 all-gather.1
Sparse Core Ops, SparseCore 1:
  96.8 46.7 reduce-scatter.1
where the time goes:
time: 183 us; the launch traced here: 182 us
  blocking collectives  129 us (70%)
  matrix products  23.9 us (13%)
  between operations  15.5 us (8%)
  local copies, waits for them, and re-layouts  7.84 us (4%)
  other arithmetic  6.04 us (3%)
    all_to_all x1, blocking collectives, on_device(): lax.all_to_all(merged, 'dp', split_axis=1, concat_axis=0, tiled=True)  64.7 us
    all_to_all x1, blocking collectives, on_device(): lax.all_to_all(outgoing, 'dp', split_axis=0, concat_axis=0, tiled=True)  26.4 us
    all_to_all x1, blocking collectives, on_device(): lax.all_to_all(slot_grad, 'dp', split_axis=0, concat_axis=0, tiled=True)  23.6 us
    psum x1, blocking collectives, on_device(): lax.psum(jnp.sum(values * values, axis=2), ('group', 'section', 'tensor'))  14.3 us
    dot_general x1, matrix products, on_device(): lax.dot_general(back, w_merge, (((1,), (1,)), ((), ())), preferred_elemen...  9.72 us
    unnamed x8, local copies, waits for them, and re-layouts  7.42 us
    dot_general x1, matrix products, on_device(): jnp.dot(placer, masked, preferred_element_type=jnp.float32)  7.02 us
    dot_general x1, matrix products, on_device(): lax.dot_general(column_block, lax.all_gather(back, 'dp', axis=0, tiled=Tr...  5.97 us
  transfers between devices with their start and end apart: 2, of which 0 were waited for; matrix products, arithmetic and copies ran while one was open for 12% of the time, Pallas kernels for 0%

commit v1 on v0

--- a/solution.py
+++ b/solution.py
@@ -32,7 +32,9 @@
     outgoing = outgoing.reshape(replicas, slots, columns)
     received = lax.all_to_all(outgoing, "dp", split_axis=0, concat_axis=0, tiled=True)
     values = received.astype(jnp.float32)
-    square_sums = lax.psum(jnp.sum(values * values, axis=2), ("group", "section", "tensor"))
+    square_sums = lax.psum(
+        lax.psum(jnp.sum(values * values, axis=2), ("section", "tensor")), "group"
+    )
     scale = lax.rsqrt(square_sums / D + 1e-05)
     normed = (values * scale[:, :, None] * norm_gain[None, None, :]).astype(jnp.bfloat16)
     embedded = normed[None]

time: 183 us -> 195 us (1.066)
  blocking collectives: 129 us -> 142 us
    psum x1 -> x3, blocking collectives: 14.3 us -> 26.3 us  [the longest x1 14.3 us: on_device(): lax.psum(jnp.sum(grad_in * values, axis=2), ('group', 'section', 'tensor'))]
  transfers between devices with their start and end apart: 2 -> 2, of which waited for: 0 -> 0; matrix products, arithmetic and copies ran while one was open for 12% -> 11% of each run, Pallas kernels for 0% -> 0%
where the time goes in v1:
time: 195 us
  blocking collectives  142 us (73%)
  matrix products  23.8 us (12%)
  between operations  15.5 us (8%)
  local copies, waits for them, and re-layouts  7.84 us (4%)
  other arithmetic  6.04 us (3%)
    all_to_all x1, blocking collectives, on_device(): lax.all_to_all(merged, 'dp', split_axis=1, concat_axis=0, tiled=True)  65.8 us
    all_to_all x1, blocking collectives, on_device(): lax.all_to_all(outgoing, 'dp', split_axis=0, concat_axis=0, tiled=True)  26.4 us
    all_to_all x1, blocking collectives, on_device(): lax.all_to_all(slot_grad, 'dp', split_axis=0, concat_axis=0, tiled=True)  23.1 us
    psum x1, blocking collectives, on_device(): lax.psum(jnp.sum(grad_in * values, axis=2), ('group', 'section', 'tensor'))  14.3 us
    dot_general x1, matrix products, on_device(): lax.dot_general(back, w_merge, (((1,), (1,)), ((), ())), preferred_elemen...  9.66 us
    psum x1, blocking collectives, on_device(): lax.psum(jnp.sum(values * values, axis=2), ('section', 'tensor'))  9.63 us
    unnamed x8, local copies, waits for them, and re-layouts  7.42 us
    dot_general x1, matrix products, on_device(): jnp.dot(placer, masked, preferred_element_type=jnp.float32)  7.02 us
  transfers between devices with their start and end apart: 2, of which 0 were waited for; matrix products, arithmetic and copies ran while one was open for 11% of the time, Pallas kernels for 0%

profile of v1, /device:TPU:0, one launch (start us, length us, event | category | flops | bytes accessed | tf_op | source)
XLA Modules:
  0.0 194.9 jit_solution(7447554740939186800)
XLA Ops:
  8.0 0.0 all-gather.2.cloned.1.call-start
  8.1 0.7 iota_compare_fusion.3
  8.7 0.7 fusion.18
  9.5 1.2 reduce-window.6
  10.8 0.1 slice.12
  10.8 0.1 copy.23
  11.0 0.1 copy.24
  11.1 0.1 add_bitcast_fusion
  11.2 0.7 fusion.16
  11.9 0.7 multiply_add_fusion
  12.5 0.0 copy-start.2
  12.5 7.0 %convolution_convert_fusion = bf16[384,1024]{1,0:T(8,128)(2,1)S(1)} fusion(bf16[192,5120]{1,0:T(8,128)(2,1)} %param.6, bf16[5120,1024]{1,0:T(8,128)(2,1)} %param.9, f32[192]{0:T(256)S(1)} %compare_convert_fusion, s32[192]{0:T(256)S(1)} %multiply_add_fusion), kind=kOutput, calls=%fused_computation.14 | convolution fusion | flops 2165514240 | bytes 13239808 | tf_op jit(solution)/shard_map/dot_general | solution.py:31
  19.6 0.0 copy-start
  19.6 26.4 %all_to_all.29 = bf16[4,96,1024]{2,1,0:T(8,128)(2,1)S(1)} all-to-all(bf16[4,96,1024]{2,1,0:T(8,128)(2,1)S(1)} %bitcast.38), channel_id=1, replica_groups=mesh['group'=2,'dp'=4,'section'=2,'tensor'=2] {'dp'}, dimensions={0} | all-to-all | bytes 1572864 | tf_op jit(solution)/shard_map/all_to_all | solution.py:33
  46.0 0.0 copy-done.2
  46.0 0.0 copy-done
  46.0 0.4 fusion.3
  46.4 14.3 %psum.23 = f32[4,96]{1,0:T(4,128)S(1)} all-reduce(f32[4,96]{1,0:T(4,128)S(1)} %get-tuple-element.18), channel_id=1, replica_groups=mesh['group'=2,'dp'=4,'section'=2,'tensor'=2] {'group','section','tensor'}, use_global_device_ids=true, to_apply=%region_8.9 | all-reduce | flops 384 | bytes 3072 | tf_op jit(solution)/shard_map/psum | solution.py:42
  60.7 9.6 %psum.21 = f32[4,96]{1,0:T(4,128)S(1)} all-reduce(f32[4,96]{1,0:T(4,128)S(1)} %get-tuple-element.19), channel_id=1, replica_groups=mesh['group'=2,'dp'=4,'section'=2,'tensor'=2] {'section','tensor'}, use_global_device_ids=true, to_apply=%region_5.6 | all-reduce | flops 384 | bytes 3072 | tf_op jit(solution)/shard_map/psum | solution.py:36
  70.3 2.5 %psum.22 = f32[4,96]{1,0:T(4,128)S(1)} all-reduce(f32[4,96]{1,0:T(4,128)S(1)} %psum.21), channel_id=1, replica_groups=mesh['group'=2,'dp'=4,'section'=2,'tensor'=2] {'group'}, use_global_device_ids=true, to_apply=%region_6.7 | all-reduce | flops 384 | bytes 3072 | tf_op jit(solution)/shard_map/psum | solution.py:35
  72.8 1.4 fusion.5
  74.2 23.1 %all_to_all.30 = bf16[4,96,1024]{2,1,0:T(8,128)(2,1)S(1)} all-to-all(bf16[4,96,1024]{2,1,0:T(8,128)(2,1)S(1)} %get-tuple-element.20), channel_id=1, replica_groups=mesh['group'=2,'dp'=4,'section'=2,'tensor'=2] {'dp'}, dimensions={0} | all-to-all | bytes 1572864 | tf_op jit(solution)/shard_map/all_to_all | solution.py:47
  97.3 1.2 fusion.7
  98.5 0.0 all-gather.2.cloned.1.call-update
  98.5 0.0 reduce-scatter.2.cloned.1.call-start
  98.5 9.7 %fusion.21 = f32[192,5120]{1,0:T(8,128)} fusion(bf16[192,1024]{1,0:T(8,128)(2,1)} %fusion.7, bf16[5120,1024]{1,0:T(8,128)(2,1)} %param.9), kind=kOutput, calls=%fused_computation.48 | convolution fusion | flops 2013265920 | bytes 14811136 | tf_op jit(solution)/shard_map/dot_general | solution.py:53
  108.2 0.0 copy-start.1
  108.2 0.0 reduce-scatter.2.cloned.1.call-update
  108.2 1.5 copy-done.1
  109.7 0.1 copy.31
  109.9 65.8 %all_to_all.31 = bf16[192,4,1280]{2,0,1:T(8,128)(2,1)S(1)} all-to-all(bf16[192,4,1280]{2,0,1:T(8,128)(2,1)S(1)} %bitcast.34), channel_id=1, replica_groups=mesh['group'=2,'dp'=4,'section'=2,'tensor'=2] {'dp'}, dimensions={1} | all-to-all | bytes 3932160 | tf_op jit(solution)/shard_map/all_to_all | solution.py:59
  175.6 0.0 all-gather.2.cloned.1.call-done
  175.6 6.0 %convolution_bitcast_fusion = f32[1280,1024]{0,1:T(8,128)} fusion(bf16[768,1024]{1,0:T(8,128)(2,1)} %all-gather.2.cloned.1.call-done, bf16[768,1280]{1,0:T(8,128)(2,1)S(1)} %bitcast.37), kind=kOutput, calls=%fused_computation | convolution fusion | flops 2013265920 | bytes 8781824 | tf_op jit(solution)/shard_map/dot_general | solution.py:60
  181.6 5.9 %copy.26 = f32[1280,1024]{1,0:T(8,128)} copy(f32[1280,1024]{0,1:T(8,128)} %convolution_bitcast_fusion) | data formatting | bytes 10485760
  187.5 0.0 reduce-scatter.2.cloned.1.call-done
  (8 shorter events, 0.1 us)
Async XLA Ops:
  8.0 167.7 %all-gather.2.cloned.1.call-start = ((), (), s32[]{:S(2)}) async-start(), calls=%async_computation.5 | async-start | bytes 1966080 | tf_op jit(solution)/shard_map/all_gather | solution.py:62
  12.5 33.4 %copy-start.2 = (f32[1024]{0:T(1024)S(1)}, f32[1024]{0:T(1024)}, u32[]{:S(2)}) copy-start(f32[1024]{0:T(1024)} %param.10) | copy-start | bytes 12292
  19.6 26.4 %copy-start = (bf16[1,4,96,1024]{3,2,1,0:T(8,128)(2,1)S(1)}, bf16[1,4,96,1024]{3,2,1,0:T(8,128)(2,1)}, u32[]{:S(2)}) copy-start(bf16[1,4,96,1024]{3,2,1,0:T(8,128)(2,1)} %param.11) | copy-start | bytes 2359300
  98.5 89.0 %reduce-scatter.2.cloned.1.call-start = ((), (), s32[]{:S(2)}) async-start(), calls=%async_computation.4 | async-start | bytes 4423680 | tf_op jit(solution)/shard_map/reduce_scatter | solution.py:56
  108.2 1.5 copy-start.1
Sparse Core Ops, SparseCore 0:
  98.6 60.6 all-gather.1
Sparse Core Ops, SparseCore 1:
  108.3 47.7 reduce-scatter.1
